TPU v7x, 32 devices: a whole 2x2x4 slice. The times are simulated.
32 devices in a mesh: groups: 2 (over y), chan: 4 (over z), tm: 2 (over core), dp: 2 (over x).
Axes of the slice: x: 2, y: 2, z: 4, core: 2. Of those that a mesh axis runs over, the one named last changes fastest.
Arguments:
- features: bfloat16 [384, 4, 8, 256], P('chan', ('groups', 'dp'), 'tm'), parts along dimension 1, may hold values from -6 to 6
- kernel: bfloat16 [384, 27, 384], P('chan'), may hold values from -0.078125 to 0.078125
- cotangent: bfloat16 [384, 4, 8, 256], P('chan', ('groups', 'dp'), 'tm'), parts along dimension 1, may hold values from -6 to 6
Outputs:
- conv_out: bfloat16 [384, 4, 8, 256], P('chan', ('groups', 'dp'), 'tm'), parts along dimension 1
- feature_grad: bfloat16 [384, 4, 8, 256], P('chan', ('groups', 'dp'), 'tm'), parts along dimension 1
- kernel_grad: float32 [768, 27, 384], P(('groups', 'chan')), parts along dimension 0
There are 2 independent parts, one for each index of `groups`. A program takes and returns all parts, laid end to end along the dimension named above; an argument that names none is the same for every part. Nothing has to cross between parts.
All inputs are finite; a program needn't handle non-finite values.
Results may differ from a plain program's by a relative error of at most 0.0051.
Values may be sent and summed in bfloat16 or wider, within the bound.
A program may use at most 128 MiB of HBM per device.

v0:
```python
import math
import jax
import jax.numpy as jnp
from jax import lax
from jax.sharding import PartitionSpec as P

WID = 64


def from_behind(x, axis, by):
    size = lax.axis_size(axis)
    pairs = [(i, i + by) for i in range(size) if 0 <= i + by < size]
    return lax.ppermute(x, axis, pairs)


def padded_copies(block):
    pixels = block.shape[-1]
    column = lax.broadcasted_iota(jnp.int32, (pixels,), 0) % WID
    nothing = jnp.zeros((), block.dtype)
    widths = [(0, 0), (0, 0), (0, 0), (WID + 1, WID + 1)]
    left_cut = jnp.pad(jnp.where(column == WID - 1, nothing, block), widths)
    untouched = jnp.pad(block, widths)
    right_cut = jnp.pad(jnp.where(column == 0, nothing, block), widths)
    return (left_cut, untouched, right_cut)


def tap_window(copies, first_frame, vertical, horizontal, frames, pixels):
    source = copies[horizontal]
    offset = vertical * WID + horizontal
    return source[:, :, first_frame : first_frame + frames, offset : offset + pixels]


def stacked_taps(copies, first_frame, flipped, frames, pixels):
    pieces = []
    for vertical in range(3):
        for horizontal in range(3):
            if flipped:
                pieces.append(
                    tap_window(copies, first_frame, 2 - vertical, 2 - horizontal, frames, pixels)
                )
            else:
                pieces.append(tap_window(copies, first_frame, vertical, horizontal, frames, pixels))
    concatenated = jnp.concatenate(pieces, axis=0)
    return concatenated.reshape(concatenated.shape[0], -1)


def local(features, kernel, cotangent):
    channels, clip_count, frames, pixels = features.shape
    flat_length = clip_count * frames * pixels
    widened = features.astype(jnp.float32)
    logistic = jax.nn.sigmoid(widened)
    activation = (widened * logistic).astype(jnp.bfloat16)
    slope_factor = logistic * (1.0 + widened * (1.0 - logistic))
    earlier = from_behind(activation[:, :, frames - 2 :, :], "tm", 1)
    extended = jnp.concatenate([earlier, activation], axis=2)
    upcoming = from_behind(cotangent[:, :, :2, :], "tm", -1)
    later_padded = jnp.concatenate([cotangent, upcoming], axis=2)
    cotangent_rows = cotangent.reshape(channels, -1)
    portion = lax.all_gather(extended, "chan", axis=0, tiled=True)
    out_sum = jnp.zeros((channels, flat_length), jnp.float32)
    amount = portion.shape[0]
    copies = padded_copies(portion)
    kernel_cols = kernel
    grad_parts = []
    for forward_temporal in range(3):
        stacked = stacked_taps(copies, forward_temporal, False, frames, pixels)
        weights = kernel_cols[:, 9 * forward_temporal : 9 * forward_temporal + 9, :].reshape(
            channels, 9 * amount
        )
        out_sum = out_sum + jnp.dot(weights, stacked, preferred_element_type=jnp.float32)
        grad_parts.append(
            lax.dot_general(
                cotangent_rows,
                stacked,
                (((1,), (1,)), ((), ())),
                preferred_element_type=jnp.float32,
            ).reshape(channels, 9, amount)
        )
    grad_sum = jnp.concatenate(grad_parts, axis=1)
    out_sum, grad_sum = (out_sum, grad_sum)
    conv_out = out_sum.reshape(features.shape).astype(jnp.bfloat16)
    position_count = lax.axis_size("dp") * lax.axis_size("tm") * flat_length
    kernel_grad = lax.psum(grad_sum, ("tm", "dp")) * (1.0 / math.sqrt(position_count))
    padded_later = padded_copies(later_padded)
    later_stacks = [
        stacked_taps(padded_later, 2 - temporal, True, frames, pixels) for temporal in range(3)
    ]
    amount = channels * lax.axis_size("chan")
    kernel_cols = kernel
    summed = jnp.zeros((amount, flat_length), jnp.float32)
    for temporal in range(3):
        weights = jnp.transpose(
            kernel_cols[:, 9 * temporal : 9 * temporal + 9, :], (2, 1, 0)
        ).reshape(amount, 9 * channels)
        summed = summed + jnp.dot(
            weights, later_stacks[temporal], preferred_element_type=jnp.float32
        )
    before_slope = lax.psum_scatter(
        summed.reshape(amount, clip_count, frames, pixels), "chan", scatter_dimension=0, tiled=True
    )
    feature_grad = (before_slope * slope_factor).astype(jnp.bfloat16)
    return (conv_out, feature_grad, kernel_grad)


def solution(mesh):
    return jax.shard_map(
        local,
        mesh=mesh,
        in_specs=(
            P("chan", ("groups", "dp"), "tm", None),
            P("chan", None, None),
            P("chan", ("groups", "dp"), "tm", None),
        ),
        out_specs=(
            P("chan", ("groups", "dp"), "tm", None),
            P("chan", ("groups", "dp"), "tm", None),
            P(("groups", "chan"), None, None),
        ),
        check_vma=False,
    )
```

profile of v0, /device:TPU:0, one launch (start us, length us, event | category | flops | bytes accessed | tf_op | source)
XLA Modules:
  0.0 263.4 jit_solution(15302708623575649266)
XLA Ops:
  9.7 1.7 fusion.80
  23.0 1.6 copy.23
  24.7 38.9 %reduce-scatter.2.cloned.1.call-done = f32[96,1,4,256]{3,0,2,1:T(8,128)} async-done(((f32[384,1,4,256]{3,0,2,1:T(8,128)}), f32[96,1,4,256]{3,0,2,1:T(8,128)}) %reduce-scatter.2.cloned.1.call-update) | async-done | bytes 393232 | tf_op jit(solution)/shard_map/reduce_scatter | solution.py:98
  63.6 1.8 fusion.48
  68.7 29.4 %all-gather.2.cloned.1.call-done = bf16[384,1,6,256]{3,0,2,1:T(8,128)(2,1)} async-done(((bf16[96,1,6,256]{3,0,2,1:T(8,128)(2,1)}), bf16[384,1,6,256]{3,0,2,1:T(8,128)(2,1)}) %all-gather.2.cloned.1.call-update) | async-done | bytes 1179664 | tf_op jit(solution)/shard_map/all_gather | solution.py:59
  102.1 1.7 fusion.31
  105.3 1.7 fusion.40
  108.5 1.6 slice_dynamic-update-slice_fusion.1
  115.7 2.9 %copy-done.1 = bf16[3456,1,4,256]{3,0,2,1:T(8,128)(2,1)} copy-done((bf16[3456,1,4,256]{3,0,2,1:T(8,128)(2,1)}, bf16[3456,1,4,256]{3,0,2,1:T(8,128)(2,1)S(1)}, u32[]{:S(2)}) %copy-start.1) | copy-done | bytes 7077912
  118.6 2.2 fusion.6
  121.4 5.2 %fusion.9 = f32[96,3456]{1,0:T(8,128)S(1)} fusion(bf16[3456,1,4,256]{3,0,2,1:T(8,128)(2,1)} %get-tuple-element.27, bf16[96,4,256]{2,1,0:T(4,128)(2,1)S(1)} %bitcast.81), kind=kOutput, calls=%fused_computation.26 | convolution fusion | flops 679477248 | bytes 8601600 | tf_op jit(solution)/shard_map/dot_general | solution.py:72
  126.6 1.8 copy.27
  128.4 6.3 %fusion.12 = f32[96,3456]{1,0:T(8,128)} fusion(bf16[3456,1,4,256]{3,0,2,1:T(8,128)(2,1)} %copy-done.2, bf16[96,4,256]{2,1,0:T(4,128)(2,1)S(1)} %bitcast.82), kind=kOutput, calls=%fused_computation.27 | convolution fusion | flops 679477248 | bytes 8601600 | tf_op jit(solution)/shard_map/dot_general | solution.py:72
  134.7 3.4 %copy.29 = f32[96,3456]{0,1:T(8,128)} copy(f32[96,3456]{1,0:T(8,128)} %fusion.12) | data formatting | bytes 2654208 | tf_op jit(solution)/shard_map/dot_general | solution.py:72
  138.1 4.3 %pad_maximum_fusion = f32[96,27,384]{0,2,1:T(8,128)} fusion(f32[96,9,384]{0,2,1:T(8,128)} %bitcast.85, f32[96,9,384]{0,2,1:T(8,128)S(1)} %bitcast.84, f32[96,9,384]{0,2,1:T(8,128)S(1)} %bitcast.83), kind=kLoop, calls=%fused_computation.6 | loop fusion | flops 1990656 | bytes 7962624 | tf_op jit(solution)/shard_map/concatenate | solution.py:79
  146.4 9.9 %copy.17 = bf16[3456,1,4,256]{0,3,2,1:T(8,128)(2,1)} copy(bf16[3456,1,4,256]{3,0,2,1:T(8,128)(2,1)} %copy-done.1) | data formatting | bytes 14155776 | tf_op jit(solution)/shard_map/concatenate | solution.py:43
  156.2 10.3 %copy.19 = bf16[3456,1,4,256]{0,3,2,1:T(8,128)(2,1)} copy(bf16[3456,1,4,256]{3,0,2,1:T(8,128)(2,1)} %get-tuple-element.27) | data formatting | bytes 14155776 | tf_op jit(solution)/shard_map/concatenate | solution.py:43
  166.6 9.7 %copy.21 = bf16[3456,1,4,256]{0,3,2,1:T(8,128)(2,1)} copy(bf16[3456,1,4,256]{3,0,2,1:T(8,128)(2,1)} %copy-done.2) | data formatting | bytes 14155776 | tf_op jit(solution)/shard_map/concatenate | solution.py:43
  176.3 5.5 %fusion.81 = f32[1024,96]{0,1:T(8,128)S(1)} fusion(bf16[3456,1024]{0,1:T(8,128)(2,1)} %bitcast.77, bf16[96,3456]{0,1:T(8,128)(2,1)S(1)} %bitcast.89), kind=kOutput, calls=%fused_computation.148 | convolution fusion | flops 679477248 | bytes 8134656 | tf_op jit(solution)/shard_map/dot_general | solution.py:70
  181.8 2.3 convolution_add_fusion.1
  184.1 2.3 fusion.16
  187.2 58.2 %all-reduce.8.cloned.1.call-done = f32[96,27,384]{0,2,1:T(8,128)} async-done(((f32[96,27,384]{0,2,1:T(8,128)}), f32[96,27,384]{0,2,1:T(8,128)}) %all-reduce.8.cloned.1.call-update) | async-done | bytes 3981328 | tf_op jit(solution)/shard_map/psum | solution.py:83
  245.5 5.4 %broadcast_multiply_fusion = f32[96,27,384]{0,2,1:T(8,128)} fusion(f32[96,27,384]{0,2,1:T(8,128)} %all-reduce.8.cloned.1.call-done), kind=kLoop, calls=%fused_computation.34 | loop fusion | flops 995328 | bytes 7962624 | tf_op jit(solution)/shard_map/mul | solution.py:83
  250.9 6.0 %copy.32 = f32[96,27,384]{2,0,1:T(8,128)} copy(f32[96,27,384]{0,2,1:T(8,128)} %broadcast_multiply_fusion) | data formatting | bytes 7962624
  (90 shorter events, 35.0 us)
Async XLA Ops:
  7.2 56.4 %reduce-scatter.2.cloned.1.call-start = ((), (), s32[]{:S(2)}) async-start(), calls=%async_computation.2 | async-start | bytes 1966080 | tf_op jit(solution)/shard_map/reduce_scatter | solution.py:98
  8.2 3.3 %copy-start.4 = (bf16[96,1,4,256]{3,2,1,0:T(4,128)(2,1)S(1)}, bf16[96,1,4,256]{3,2,1,0:T(4,128)(2,1)}, u32[]{:S(2)}) copy-start(bf16[96,1,4,256]{3,2,1,0:T(4,128)(2,1)} %param.5) | copy-start | bytes 589828
  8.2 3.3 %collective-permute-start.1 = (bf16[96,1,2,256]{3,2,1,0:T(2,128)(2,1)S(1)}, bf16[96,1,2,256]{3,2,1,0:T(2,128)(2,1)S(1)}, u32[]{:S(2)}, u32[]{:S(2)}) collective-permute-start(bf16[96,1,2,256]{3,2,1,0:T(2,128)(2,1)S(1)} %slice.215), channel_id=1, source_target_pairs={{2,0},{3,1},{6,4},{7,5},{10,8},{11,9},{14,12},{15,13},{18,16},{19,... | collective-permute-start | bytes 294920 | tf_op jit(solution)/shard_map/ppermute | solution.py:13
  11.4 7.8 %copy-start.10 = (bf16[96,9,384]{2,0,1:T(8,128)(2,1)}, bf16[96,9,384]{2,0,1:T(8,128)(2,1)S(1)}, u32[]{:S(2)}) copy-start(bf16[96,9,384]{2,0,1:T(8,128)(2,1)S(1)} %get-tuple-element.10) | copy-start | bytes 1990660
  11.4 9.0 %copy-start.8 = (bf16[96,9,384]{2,0,1:T(8,128)(2,1)}, bf16[96,9,384]{2,0,1:T(8,128)(2,1)S(1)}, u32[]{:S(2)}) copy-start(bf16[96,9,384]{2,0,1:T(8,128)(2,1)S(1)} %get-tuple-element.11) | copy-start | bytes 1990660
  11.4 10.3 %copy-start.6 = (bf16[96,9,384]{2,0,1:T(8,128)(2,1)}, bf16[96,9,384]{2,0,1:T(8,128)(2,1)S(1)}, u32[]{:S(2)}) copy-start(bf16[96,9,384]{2,0,1:T(8,128)(2,1)S(1)} %get-tuple-element.9) | copy-start | bytes 1990660
  23.0 40.6 %copy-start.13 = (bf16[96,1,4,256]{3,2,1,0:T(4,128)(2,1)S(1)}, bf16[96,1,4,256]{3,2,1,0:T(4,128)(2,1)}, u32[]{:S(2)}) copy-start(bf16[96,1,4,256]{3,2,1,0:T(4,128)(2,1)} %param.3) | copy-start | bytes 589828
  24.6 73.5 %all-gather.2.cloned.1.call-start = ((), (), s32[]{:S(2)}) async-start(), calls=%async_computation.1 | async-start | bytes 1474560 | tf_op jit(solution)/shard_map/all_gather | solution.py:59
  65.4 2.3 collective-permute-start
  68.5 177.0 %all-reduce.8.cloned.1.call-start = ((), (), s32[]{:S(2)}) async-start(), calls=%async_computation.3 | async-start | bytes 10616832 | tf_op jit(solution)/shard_map/psum | solution.py:83
  98.1 1.8 copy-start
  107.0 8.6 %copy-start.2 = (bf16[3456,1,4,256]{3,0,2,1:T(8,128)(2,1)}, bf16[3456,1,4,256]{3,0,2,1:T(8,128)(2,1)S(1)}, u32[]{:S(2)}) copy-start(bf16[3456,1,4,256]{3,0,2,1:T(8,128)(2,1)S(1)} %get-tuple-element.12) | copy-start | bytes 21233668
  115.7 2.9 %copy-start.1 = (bf16[3456,1,4,256]{3,0,2,1:T(8,128)(2,1)}, bf16[3456,1,4,256]{3,0,2,1:T(8,128)(2,1)S(1)}, u32[]{:S(2)}) copy-start(bf16[3456,1,4,256]{3,0,2,1:T(8,128)(2,1)S(1)} %get-tuple-element.28) | copy-start | bytes 21233668
  134.7 3.4 %copy-start.5 = (f32[96,3456]{0,1:T(8,128)S(1)}, f32[96,3456]{0,1:T(8,128)}, u32[]{:S(2)}) copy-start(f32[96,3456]{0,1:T(8,128)} %copy.27) | copy-start | bytes 3981316
  142.4 1.1 copy-start.11
  143.5 1.1 copy-start.9
  143.5 1.5 copy-start.7
  143.5 2.0 copy-start.12
  176.3 5.5 %copy-start.3 = (bf16[3456,1,4,256]{0,3,2,1:T(8,128)(2,1)S(1)}, bf16[3456,1,4,256]{0,3,2,1:T(8,128)(2,1)}, u32[]{:S(2)}) copy-start(bf16[3456,1,4,256]{0,3,2,1:T(8,128)(2,1)} %copy.19) | copy-start | bytes 21233668
  176.3 7.8 %slice-start = ((s8[7077888]{0:T(1024)(128)(4,1)}), s8[4194304]{0:T(1024)(128)(4,1)S(1)}, s32[]{:S(2)}) async-start(s8[7077888]{0:T(1024)(128)(4,1)} %bitcast.73), calls=%async_computation.4 | async-start | bytes 8388608
  181.8 2.3 slice-start.1
Sparse Core Ops, SparseCore 0:
  24.7 38.8 reduce-scatter.1
  68.6 29.4 all-gather.1
  142.6 102.8 all-reduce.7
where the time goes:
time: 265 us; the launch traced here: 263 us
  waiting for transfers between devices  128 us (48%)
  local copies, waits for them, and re-layouts  76.3 us (29%)
  matrix products  27.6 us (10%)
  other arithmetic  14.7 us (6%)
  between operations  14.1 us (5%)
  starting transfers between devices  3.09 us (1%)
    psum x1, waiting for transfers between devices, local(): lax.psum(grad_sum, ('tm', 'dp')) * (1.0 / math.sqrt(position_count))  58.2 us
    reduce_scatter x1, waiting for transfers between devices, local(): lax.psum_scatter(summed.reshape(amount, clip_count, frames, pixels), 'cha...  38.9 us
    concatenate x7, local copies, waits for them, and re-layouts, stacked_taps(): concatenated = jnp.concatenate(pieces, axis=0)  34.2 us
    unnamed x64, local copies, waits for them, and re-layouts  29.9 us
    all_gather x1, waiting for transfers between devices, local(): portion = lax.all_gather(extended, 'chan', axis=0, tiled=True)  29.4 us
    dot_general x3, matrix products, local(): lax.dot_general(cotangent_rows, stacked, (((1,), (1,)), ((), ())), prefer...  13.8 us
    dot_general x3, matrix products, local(): jnp.dot(weights, stacked, preferred_element_type=jnp.float32)  10 us
    dot_general x3, local copies, waits for them, and re-layouts, local(): lax.dot_general(cotangent_rows, stacked, (((1,), (1,)), ((), ())), prefer...  5.72 us
  transfers between devices with their start and end apart: 5, of which 5 were waited for; matrix products, arithmetic and copies ran while one was open for 17% of the time, Pallas kernels for 0%

commit v1 on v0

--- a/solution.py
+++ b/solution.py
@@ -5,6 +5,17 @@
 from jax.sharding import PartitionSpec as P
 
 WID = 64
+
+
+def pass_along(array, name, dim):
+    size = lax.axis_size(name)
+    right = [(i, (i + 1) % size) for i in range(size)]
+    pieces = [array]
+    for hop in range(1, size):
+        pieces = [lax.ppermute(pieces[0], name, right), *pieces]
+    out = jnp.concatenate(pieces, axis=dim)
+    shift = (lax.axis_index(name) + 1) * pieces[-1].shape[dim]
+    return jnp.roll(out, shift, axis=dim)
 
 
 def from_behind(x, axis, by):
@@ -56,7 +67,7 @@
     upcoming = from_behind(cotangent[:, :, :2, :], "tm", -1)
     later_padded = jnp.concatenate([cotangent, upcoming], axis=2)
     cotangent_rows = cotangent.reshape(channels, -1)
-    portion = lax.all_gather(extended, "chan", axis=0, tiled=True)
+    portion = pass_along(extended, "chan", 0)
     out_sum = jnp.zeros((channels, flat_length), jnp.float32)
     amount = portion.shape[0]
     copies = padded_copies(portion)

time: 265 us -> 270 us (1.019)
  local copies, waits for them, and re-layouts: 76.3 us -> 83.3 us
    ppermute x0 -> x3, waiting for transfers between devices: none -> 30.5 us  [pass_along(): pieces = [lax.ppermute(pieces[0], name, right), *pieces]]
    all_gather x1 -> x0, waiting for transfers between devices: 29.4 us -> none  [local(): portion = lax.all_gather(extended, 'chan', axis=0, tiled=True)]
    unnamed x64 -> x66, local copies, waits for them, and re-layouts: 29.9 us -> 35.6 us
  transfers between devices with their start and end apart: 5 -> 7, of which waited for: 5 -> 7; matrix products, arithmetic and copies ran while one was open for 17% -> 17% of each run, Pallas kernels for 0% -> 0%
where the time goes in v1:
time: 270 us; the launch traced here: 268 us
  waiting for transfers between devices  127 us (47%)
  local copies, waits for them, and re-layouts  83.3 us (31%)
  matrix products  27.6 us (10%)
  between operations  14.4 us (5%)
  other arithmetic  13 us (5%)
  starting transfers between devices  2.89 us (1%)
    psum x1, waiting for transfers between devices, local(): lax.psum(grad_sum, ('tm', 'dp')) * (1.0 / math.sqrt(position_count))  56.7 us
    reduce_scatter x1, waiting for transfers between devices, local(): lax.psum_scatter(summed.reshape(amount, clip_count, frames, pixels), 'cha...  38.9 us
    unnamed x66, local copies, waits for them, and re-layouts  35.6 us
    concatenate x7, local copies, waits for them, and re-layouts, stacked_taps(): concatenated = jnp.concatenate(pieces, axis=0)  35.4 us
    ppermute x3, waiting for transfers between devices, pass_along(): pieces = [lax.ppermute(pieces[0], name, right), *pieces]  30.5 us
    dot_general x3, matrix products, local(): lax.dot_general(cotangent_rows, stacked, (((1,), (1,)), ((), ())), prefer...  13.8 us
    dot_general x3, matrix products, local(): jnp.dot(weights, stacked, preferred_element_type=jnp.float32)  10 us
    dot_general x3, local copies, waits for them, and re-layouts, local(): lax.dot_general(cotangent_rows, stacked, (((1,), (1,)), ((), ())), prefer...  5.78 us
  transfers between devices with their start and end apart: 7, of which 7 were waited for; matrix products, arithmetic and copies ran while one was open for 17% of the time, Pallas kernels for 0%

profile of v1, /device:TPU:0, one launch (start us, length us, event | category | flops | bytes accessed | tf_op | source)
XLA Modules:
  0.0 268.4 jit_solution(7460760572952312745)
XLA Ops:
  24.6 38.9 %reduce-scatter.2.cloned.1.call-done = f32[96,1,4,256]{3,0,2,1:T(8,128)} async-done(((f32[384,1,4,256]{3,0,2,1:T(8,128)}), f32[96,1,4,256]{3,0,2,1:T(8,128)}) %reduce-scatter.2.cloned.1.call-update) | async-done | bytes 393232 | tf_op jit(solution)/shard_map/reduce_scatter | solution.py:109
  63.5 1.8 fusion.48
  67.8 11.0 %collective-permute-done.1 = bf16[96,1,6,256]{3,0,2,1:T(8,128)(2,1)S(1)} collective-permute-done((bf16[96,1,6,256]{3,0,2,1:T(8,128)(2,1)S(1)}, bf16[96,1,6,256]{3,0,2,1:T(8,128)(2,1)S(1)}, u32[]{:S(2)}, u32[]{:S(2)}) %collective-permute-start.1) | collective-permute-done | bytes 294944 | tf_op jit(solution)/shard_map/ppermute | solution.py:15
  78.8 10.2 %collective-permute-done.2 = bf16[96,1,6,256]{3,0,2,1:T(8,128)(2,1)S(1)} collective-permute-done((bf16[96,1,6,256]{3,0,2,1:T(8,128)(2,1)S(1)}, bf16[96,1,6,256]{3,0,2,1:T(8,128)(2,1)S(1)}, u32[]{:S(2)}, u32[]{:S(2)}) %collective-permute-start.2) | collective-permute-done | bytes 294944 | tf_op jit(solution)/shard_map/ppermute | solution.py:15
  89.0 9.4 %collective-permute-done.3 = bf16[96,1,6,256]{3,0,2,1:T(8,128)(2,1)S(1)} collective-permute-done((bf16[96,1,6,256]{3,0,2,1:T(8,128)(2,1)S(1)}, bf16[96,1,6,256]{3,0,2,1:T(8,128)(2,1)S(1)}, u32[]{:S(2)}, u32[]{:S(2)}) %collective-permute-start.3) | collective-permute-done | bytes 294944 | tf_op jit(solution)/shard_map/ppermute | solution.py:15
  103.6 2.0 fusion.30
  109.2 2.2 dynamic-slice_dynamic-update-slice_fusion
  115.1 2.0 fusion.40
  121.5 2.9 %copy-done = bf16[3456,1,4,256]{3,0,2,1:T(8,128)(2,1)} copy-done((bf16[3456,1,4,256]{3,0,2,1:T(8,128)(2,1)}, bf16[3456,1,4,256]{3,0,2,1:T(8,128)(2,1)S(1)}, u32[]{:S(2)}) %copy-start) | copy-done | bytes 7077912
  124.3 2.2 fusion.6
  127.1 5.2 %fusion.9 = f32[96,3456]{1,0:T(8,128)S(1)} fusion(bf16[3456,1,4,256]{3,0,2,1:T(8,128)(2,1)} %get-tuple-element.29, bf16[96,4,256]{2,1,0:T(4,128)(2,1)S(1)} %bitcast.81), kind=kOutput, calls=%fused_computation.26 | convolution fusion | flops 679477248 | bytes 8601600 | tf_op jit(solution)/shard_map/dot_general | solution.py:83
  132.3 2.0 copy.27
  134.4 6.3 %fusion.12 = f32[96,3456]{1,0:T(8,128)} fusion(bf16[3456,1,4,256]{3,0,2,1:T(8,128)(2,1)} %get-tuple-element.17, bf16[96,4,256]{2,1,0:T(4,128)(2,1)S(1)} %bitcast.82), kind=kOutput, calls=%fused_computation.27 | convolution fusion | flops 679477248 | bytes 8601600 | tf_op jit(solution)/shard_map/dot_general | solution.py:83
  140.7 3.2 %copy.29 = f32[96,3456]{0,1:T(8,128)} copy(f32[96,3456]{1,0:T(8,128)} %fusion.12) | data formatting | bytes 2654208 | tf_op jit(solution)/shard_map/dot_general | solution.py:83
  143.9 4.3 %pad_maximum_fusion = f32[96,27,384]{0,2,1:T(8,128)} fusion(f32[96,9,384]{0,2,1:T(8,128)} %bitcast.85, f32[96,9,384]{0,2,1:T(8,128)S(1)} %bitcast.84, f32[96,9,384]{0,2,1:T(8,128)S(1)} %bitcast.83), kind=kLoop, calls=%fused_computation.6 | loop fusion | flops 1990656 | bytes 7962624 | tf_op jit(solution)/shard_map/concatenate | solution.py:90
  151.7 10.5 %copy.17 = bf16[3456,1,4,256]{0,3,2,1:T(8,128)(2,1)} copy(bf16[3456,1,4,256]{3,0,2,1:T(8,128)(2,1)} %copy-done) | data formatting | bytes 14155776 | tf_op jit(solution)/shard_map/concatenate | solution.py:54
  162.2 10.4 %copy.19 = bf16[3456,1,4,256]{0,3,2,1:T(8,128)(2,1)} copy(bf16[3456,1,4,256]{3,0,2,1:T(8,128)(2,1)} %get-tuple-element.29) | data formatting | bytes 14155776 | tf_op jit(solution)/shard_map/concatenate | solution.py:54
  172.6 9.9 %copy.21 = bf16[3456,1,4,256]{0,3,2,1:T(8,128)(2,1)} copy(bf16[3456,1,4,256]{3,0,2,1:T(8,128)(2,1)} %get-tuple-element.17) | data formatting | bytes 14155776 | tf_op jit(solution)/shard_map/concatenate | solution.py:54
  182.6 5.5 %fusion.81 = f32[1024,96]{0,1:T(8,128)S(1)} fusion(bf16[3456,1024]{0,1:T(8,128)(2,1)} %bitcast.77, bf16[96,3456]{0,1:T(8,128)(2,1)S(1)} %bitcast.89), kind=kOutput, calls=%fused_computation.157 | convolution fusion | flops 679477248 | bytes 8134656 | tf_op jit(solution)/shard_map/dot_general | solution.py:81
  188.0 2.3 convolution_add_fusion.1
  190.4 2.3 fusion.16
  193.5 56.7 %all-reduce.8.cloned.1.call-done = f32[96,27,384]{0,2,1:T(8,128)} async-done(((f32[96,27,384]{0,2,1:T(8,128)}), f32[96,27,384]{0,2,1:T(8,128)}) %all-reduce.8.cloned.1.call-update) | async-done | bytes 3981328 | tf_op jit(solution)/shard_map/psum | solution.py:94
  250.1 5.4 %broadcast_multiply_fusion = f32[96,27,384]{0,2,1:T(8,128)} fusion(f32[96,27,384]{0,2,1:T(8,128)} %all-reduce.8.cloned.1.call-done), kind=kLoop, calls=%fused_computation.34 | loop fusion | flops 995328 | bytes 7962624 | tf_op jit(solution)/shard_map/mul | solution.py:94
  255.6 6.0 %copy.32 = f32[96,27,384]{2,0,1:T(8,128)} copy(f32[96,27,384]{0,2,1:T(8,128)} %broadcast_multiply_fusion) | data formatting | bytes 7962624
  (98 shorter events, 41.3 us)
Async XLA Ops:
  7.2 4.3 %copy-start.2 = (bf16[96,1,4,256]{3,2,1,0:T(4,128)(2,1)S(1)}, bf16[96,1,4,256]{3,2,1,0:T(4,128)(2,1)}, u32[]{:S(2)}) copy-start(bf16[96,1,4,256]{3,2,1,0:T(4,128)(2,1)} %param.5) | copy-start | bytes 589828
  7.2 56.3 %reduce-scatter.2.cloned.1.call-start = ((), (), s32[]{:S(2)}) async-start(), calls=%async_computation.1 | async-start | bytes 1966080 | tf_op jit(solution)/shard_map/reduce_scatter | solution.py:109
  8.3 3.2 %collective-permute-start.4 = (bf16[96,1,2,256]{3,2,1,0:T(2,128)(2,1)S(1)}, bf16[96,1,2,256]{3,2,1,0:T(2,128)(2,1)S(1)}, u32[]{:S(2)}, u32[]{:S(2)}) collective-permute-start(bf16[96,1,2,256]{3,2,1,0:T(2,128)(2,1)S(1)} %slice.215), channel_id=1, source_target_pairs={{2,0},{3,1},{6,4},{7,5},{10,8},{11,9},{14,12},{15,13},{18,16},{19,... | collective-permute-start | bytes 294920 | tf_op jit(solution)/shard_map/ppermute | solution.py:24
  11.3 7.8 %copy-start.8 = (bf16[96,9,384]{2,0,1:T(8,128)(2,1)}, bf16[96,9,384]{2,0,1:T(8,128)(2,1)S(1)}, u32[]{:S(2)}) copy-start(bf16[96,9,384]{2,0,1:T(8,128)(2,1)S(1)} %get-tuple-element.15) | copy-start | bytes 1990660
  11.3 9.0 %copy-start.6 = (bf16[96,9,384]{2,0,1:T(8,128)(2,1)}, bf16[96,9,384]{2,0,1:T(8,128)(2,1)S(1)}, u32[]{:S(2)}) copy-start(bf16[96,9,384]{2,0,1:T(8,128)(2,1)S(1)} %get-tuple-element.16) | copy-start | bytes 1990660
  11.3 10.3 %copy-start.4 = (bf16[96,9,384]{2,0,1:T(8,128)(2,1)}, bf16[96,9,384]{2,0,1:T(8,128)(2,1)S(1)}, u32[]{:S(2)}) copy-start(bf16[96,9,384]{2,0,1:T(8,128)(2,1)S(1)} %get-tuple-element.14) | copy-start | bytes 1990660
  22.9 40.6 %copy-start.11 = (bf16[96,1,4,256]{3,2,1,0:T(4,128)(2,1)S(1)}, bf16[96,1,4,256]{3,2,1,0:T(4,128)(2,1)}, u32[]{:S(2)}) copy-start(bf16[96,1,4,256]{3,2,1,0:T(4,128)(2,1)} %param.3) | copy-start | bytes 589828
  24.5 225.6 %all-reduce.8.cloned.1.call-start = ((), (), s32[]{:S(2)}) async-start(), calls=%async_computation.2 | async-start | bytes 10616832 | tf_op jit(solution)/shard_map/psum | solution.py:94
  65.3 2.3 collective-permute-start
  67.7 11.1 %collective-permute-start.1 = (bf16[96,1,6,256]{3,0,2,1:T(8,128)(2,1)S(1)}, bf16[96,1,6,256]{3,0,2,1:T(8,128)(2,1)S(1)}, u32[]{:S(2)}, u32[]{:S(2)}) collective-permute-start(bf16[96,1,6,256]{3,0,2,1:T(8,128)(2,1)S(1)} %pad_maximum_fusion.2), channel_id=1, source_target_pairs={{0,4},{4,8},{8,12},{12,0},{1,5},{5,9},{9,13},{13,1},{2,6},{6,10},{... | collective-permute-start | bytes 884744 | tf_op jit(solution)/shard_map/ppermute | solution.py:15
  78.8 10.2 %collective-permute-start.2 = (bf16[96,1,6,256]{3,0,2,1:T(8,128)(2,1)S(1)}, bf16[96,1,6,256]{3,0,2,1:T(8,128)(2,1)S(1)}, u32[]{:S(2)}, u32[]{:S(2)}) collective-permute-start(bf16[96,1,6,256]{3,0,2,1:T(8,128)(2,1)S(1)} %collective-permute-done.1), channel_id=1, source_target_pairs={{0,4},{4,8},{8,12},{12,0},{1,5},{5,9},{9,13},{13,1},{2,6},{6,10},{... | collective-permute-start | bytes 884744 | tf_op jit(solution)/shard_map/ppermute | solution.py:15
  89.0 9.4 %collective-permute-start.3 = (bf16[96,1,6,256]{3,0,2,1:T(8,128)(2,1)S(1)}, bf16[96,1,6,256]{3,0,2,1:T(8,128)(2,1)S(1)}, u32[]{:S(2)}, u32[]{:S(2)}) collective-permute-start(bf16[96,1,6,256]{3,0,2,1:T(8,128)(2,1)S(1)} %collective-permute-done.2), channel_id=1, source_target_pairs={{0,4},{4,8},{8,12},{12,0},{1,5},{5,9},{9,13},{13,1},{2,6},{6,10},{... | collective-permute-start | bytes 884744 | tf_op jit(solution)/shard_map/ppermute | solution.py:15
  121.4 2.9 %copy-start = (bf16[3456,1,4,256]{3,0,2,1:T(8,128)(2,1)}, bf16[3456,1,4,256]{3,0,2,1:T(8,128)(2,1)S(1)}, u32[]{:S(2)}) copy-start(bf16[3456,1,4,256]{3,0,2,1:T(8,128)(2,1)S(1)} %get-tuple-element.30) | copy-start | bytes 21233668
  140.7 3.2 %copy-start.3 = (f32[96,3456]{0,1:T(8,128)S(1)}, f32[96,3456]{0,1:T(8,128)}, u32[]{:S(2)}) copy-start(f32[96,3456]{0,1:T(8,128)} %copy.27) | copy-start | bytes 3981316
  148.2 1.1 copy-start.9
  148.2 1.5 copy-start.7
  149.3 1.1 copy-start.5
  149.3 1.6 copy-start.10
  182.6 5.5 %copy-start.1 = (bf16[3456,1,4,256]{0,3,2,1:T(8,128)(2,1)S(1)}, bf16[3456,1,4,256]{0,3,2,1:T(8,128)(2,1)}, u32[]{:S(2)}) copy-start(bf16[3456,1,4,256]{0,3,2,1:T(8,128)(2,1)} %copy.19) | copy-start | bytes 21233668
  182.6 7.8 %slice-start = ((s8[7077888]{0:T(1024)(128)(4,1)}), s8[4194304]{0:T(1024)(128)(4,1)S(1)}, s32[]{:S(2)}) async-start(s8[7077888]{0:T(1024)(128)(4,1)} %bitcast.73), calls=%async_computation.3 | async-start | bytes 8388608
  188.0 2.3 slice-start.1
Sparse Core Ops, SparseCore 0:
  24.6 38.8 reduce-scatter.1
  148.4 101.7 all-reduce.7
